TPU v7x, 512 devices: a whole 4x8x8 slice. The times are simulated.
512 devices in a mesh: seq: 128 (over x, z, y_hi), tp: 4 (over y_lo, core).
Axes of the slice: x: 4, y: 8 (y_hi: 4, y_lo: 2; y = y_hi * 2 + y_lo), z: 8, core: 2. Of those that a mesh axis runs over, the one named last changes fastest.
Arguments:
- residual_in: float32 [32768, 2048], P('seq', 'tp'), may hold values from -18 to 18
- query_rows: bfloat16 [32768, 2048], P('seq', 'tp'), may hold values from -6 to 6
- key_rows: bfloat16 [32768, 2048], P('seq', 'tp'), may hold values from -6 to 6
- value_rows: bfloat16 [32768, 2048], P('seq', 'tp'), may hold values from -6 to 6
- lengths: int32 [256], P('seq'), may hold values from 0 to 128, as said below
- norm_gain: float32 [2048], P('tp'), may hold values from 0.1 to 1.9
- gate_weight: bfloat16 [2048, 4096], P('seq', 'tp'), may hold values from -0.125 to 0.125
- up_weight: bfloat16 [2048, 4096], P('seq', 'tp'), may hold values from -0.125 to 0.125
- down_weight: bfloat16 [4096, 2048], P('tp', 'seq'), may hold values from -0.375 to 0.375
Outputs:
- attended: bfloat16 [32768, 2048], P('seq', 'tp')
- mixed: float32 [32768, 2048], P('seq', 'tp')
Inputs may be any that keep to these rules, and one draw needn't show every extreme that they name: `lengths`: entry s counts the valid events at the start of segment s, the events s * 128 to s * 128 + 127; the rest of the segment is padding.
All inputs are finite; a program needn't handle non-finite values.
Results may differ from a plain program's by a relative error of at most 0.008.
Values may be sent and summed in bfloat16 or wider, within the bound.
No kernel may reach another device: no remote copies, remote signals or barrier semaphores. Data moves between devices by JAX's collectives and lax.ppermute only.
A program may use at most 64 MiB of HBM per device.

v0:
```python
import math
import jax
import jax.numpy as jnp
from jax import lax
from jax.sharding import PartitionSpec as P

D = 2048
HEAD_DIM = 128
SEG = 128
WINDOW = 512
epsilon = 1e-06


def from_behind(value, axis, by):
    size = lax.axis_size(axis)
    pairs = [(i, i + by) for i in range(size) if 0 <= i + by < size]
    return lax.ppermute(value, axis, pairs)


def on_device(
    residual_in,
    query_rows,
    key_rows,
    value_rows,
    lengths,
    norm_gain,
    gate_weight,
    up_weight,
    down_weight,
):
    row_count = query_rows.shape[0]
    head_local = query_rows.shape[1] // HEAD_DIM
    reach_blocks = (WINDOW + row_count - 2) // row_count
    seq_index = lax.axis_index("seq")
    offsets = jnp.arange(row_count, dtype=jnp.int32) % SEG
    own_valid = (offsets < jnp.repeat(lengths, SEG, total_repeat_length=row_count)).astype(
        jnp.bfloat16
    )
    previous = from_behind((key_rows, value_rows, own_valid), "seq", 1)
    earlier = [previous]
    earlier.append(from_behind((key_rows, value_rows, own_valid), "seq", 2))
    oldest_first = earlier[::-1]
    key_window = jnp.concatenate([block[0] for block in oldest_first] + [key_rows], axis=0)
    value_window = jnp.concatenate([block[1] for block in oldest_first] + [value_rows], axis=0)
    valid_window = jnp.concatenate([block[2] for block in oldest_first] + [own_valid], axis=0)
    key_span = key_window.shape[0]
    query_pos = seq_index * row_count + jnp.arange(row_count, dtype=jnp.int32)
    key_pos = (seq_index - reach_blocks) * row_count + jnp.arange(key_span, dtype=jnp.int32)
    allowed = (key_pos[None, :] <= query_pos[:, None]) & (
        key_pos[None, :] > query_pos[:, None] - WINDOW
    )
    allowed = allowed & (key_pos[None, :] >= 0) & (valid_window[None, :] > 0)
    keep_rows = (own_valid > 0)[:, None]
    score_scale = 1.0 / math.sqrt(HEAD_DIM)
    outputs = []
    for head_index in range(head_local):
        low_col = head_index * HEAD_DIM
        query_head = query_rows[:, low_col : low_col + HEAD_DIM]
        key_head = key_window[:, low_col : low_col + HEAD_DIM]
        value_head = value_window[:, low_col : low_col + HEAD_DIM]
        scores = (
            lax.dot_general(
                query_head, key_head, (((1,), (1,)), ((), ())), preferred_element_type=jnp.float32
            )
            * score_scale
        )
        masked = jnp.where(allowed, scores, -1e30)
        row_max = jnp.max(masked, axis=1, keepdims=True)
        weights = jnp.where(allowed, jnp.exp(masked - row_max), 0.0)
        denominator = jnp.sum(weights, axis=1, keepdims=True)
        numerator = jnp.dot(
            weights.astype(jnp.bfloat16), value_head, preferred_element_type=jnp.float32
        )
        outputs.append(
            jnp.where(keep_rows, numerator / jnp.where(keep_rows, denominator, 1.0), 0.0)
        )
    attended = jnp.concatenate(outputs, axis=1).astype(jnp.bfloat16)
    residual = residual_in + attended.astype(jnp.float32)
    square_sum = lax.psum(jnp.sum(residual * residual, axis=1), "tp")
    inverse = lax.rsqrt(square_sum / D + epsilon)
    normed = (residual * inverse[:, None] * norm_gain[None, :]).astype(jnp.bfloat16)
    normed_full = lax.all_gather(normed, "tp", axis=1, tiled=True)
    gate_full, up_full = (
        lax.all_gather(gate_weight, "seq", axis=0, tiled=True),
        lax.all_gather(up_weight, "seq", axis=0, tiled=True),
    )
    gate_sum = jnp.dot(normed_full, gate_full, preferred_element_type=jnp.float32)
    up_sum = jnp.dot(normed_full, up_full, preferred_element_type=jnp.float32)
    hidden = (jax.nn.silu(gate_sum) * up_sum).astype(jnp.bfloat16)
    down_full = lax.all_gather(down_weight, "seq", axis=1, tiled=True)
    partial_value = jnp.dot(hidden, down_full, preferred_element_type=jnp.float32)
    tp_width = residual_in.shape[1]
    summed = lax.psum(partial_value.astype(jnp.bfloat16), "tp").astype(jnp.float32)
    branch_share = lax.dynamic_slice_in_dim(summed, lax.axis_index("tp") * tp_width, tp_width, 1)
    mixed = residual + branch_share
    return (attended, mixed)


def solution(mesh):
    placed = (
        P("seq", "tp"),
        P("seq", "tp"),
        P("seq", "tp"),
        P("seq", "tp"),
        P("seq"),
        P("tp"),
        P("seq", "tp"),
        P("seq", "tp"),
        P("tp", "seq"),
    )
    return jax.shard_map(
        on_device,
        mesh=mesh,
        in_specs=placed,
        out_specs=(P("seq", "tp"), P("seq", "tp")),
        check_vma=False,
    )
```

profile of v0, /device:TPU:1, one launch (start us, length us, event | category | flops | bytes accessed | tf_op | source)
XLA Modules:
  0.0 574.4 jit_solution(10562217400988549649)
XLA Ops:
  7.2 0.0 copy-start.3
  7.2 0.0 all-gather.5.cloned.1.call-start
  7.2 1.3 fusion.57
  8.6 1.3 compare_select_fusion.1
  9.9 8.3 %collective-permute-start = (bf16[256]{0:T(256)(128)(2,1)S(1)}, bf16[256]{0:T(256)(128)(2,1)S(1)}, u32[]{:S(2)}, u32[]{:S(2)}) collective-permute-start(bf16[256]{0:T(256)(128)(2,1)S(1)} %get-tuple-element.21), channel_id=1, source_target_pairs={{0,8},{4,12},{8,16},{12,20},{16,24},{20,28},{24,32},{28,36},{32,40... | collective-permute-start | bytes 1544 | tf_op jit(solution)/shard_map/ppermute | solution.py:17
  18.2 2.4 collective-permute-start.1
  20.6 5.4 collective-permute-start.2
  26.0 5.4 collective-permute-start.3
  31.4 3.5 collective-permute-start.4
  35.0 1.2 copy.11
  36.3 0.0 collective-permute-done
  36.3 4.2 collective-permute-start.5
  40.5 0.0 collective-permute-done.1
  40.5 0.0 collective-permute-done.2
  40.6 2.4 collective-permute-done.3
  43.0 1.0 constant_dynamic-update-slice_fusion
  43.9 0.0 copy-start
  43.9 1.3 fusion.59
  45.2 0.0 copy-done.3
  45.3 0.4 fusion.60
  45.7 0.4 fusion.61
  46.1 3.1 collective-permute-done.4
  49.2 0.4 fusion.58
  49.6 10.2 %collective-permute-done.5 = bf16[256,512]{1,0:T(8,128)(2,1)S(1)} collective-permute-done((bf16[256,512]{1,0:T(8,128)(2,1)}, bf16[256,512]{1,0:T(8,128)(2,1)S(1)}, u32[]{:S(2)}, u32[]{:S(2)}) %collective-permute-start.5) | collective-permute-done | bytes 262176 | tf_op jit(solution)/shard_map/ppermute | solution.py:17
  59.8 0.0 copy-done
  59.8 1.0 fusion.17
  60.9 0.6 fusion.13
  61.5 0.0 copy-start.1
  61.5 0.6 fusion.14
  62.1 0.6 fusion.15
  62.8 0.6 fusion.16
  63.4 0.1 multiply_reduce_fusion
  63.5 17.3 %psum.14 = f32[256]{0:T(256)S(1)} all-reduce(f32[256]{0:T(256)S(1)} %multiply_reduce_fusion), channel_id=1, replica_groups=mesh['seq'=128,'tp'=4] {'tp'}, use_global_device_ids=true, to_apply=%region_9.10 | all-reduce | flops 256 | bytes 2048 | tf_op jit(solution)/shard_map/psum | solution.py:79
  80.7 0.0 copy-done.1
  80.8 0.8 multiply_convert_fusion
  81.6 0.0 all-gather.5.cloned.1.call-update
  81.6 0.0 all-gather.7.cloned.1.call-start
  81.7 0.7 all-gather.7.cloned.1.call-update
  82.4 0.0 all-gather.11.cloned.1.call-start
  82.4 0.7 all-gather.11.cloned.1.call-update
  83.1 0.0 all-gather.9.cloned.1.call-start
  83.2 0.5 all-gather.9.cloned.1.call-update
  83.7 0.0 all-reduce.2.cloned.1.call-start
  83.7 29.9 %all-gather.5.cloned.1.call-done = bf16[256,2048]{0,1:T(8,128)(2,1)} async-done(((bf16[256,512]{0,1:T(8,128)(2,1)}), bf16[256,2048]{0,1:T(8,128)(2,1)}) %all-gather.5.cloned.1.call-update) | async-done | bytes 1048592 | tf_op jit(solution)/shard_map/all_gather | solution.py:82
  113.7 0.0 copy-start.2
  113.7 132.3 %all-gather.7.cloned.1.call-done = bf16[2048,1024]{1,0:T(8,128)(2,1)} async-done(((bf16[16,1024]{1,0:T(8,128)(2,1)}), bf16[2048,1024]{1,0:T(8,128)(2,1)}) %all-gather.7.cloned.1.call-update) | async-done | bytes 4194320 | tf_op jit(solution)/shard_map/all_gather | solution.py:84
  245.9 3.8 fusion.62
  249.7 127.1 %all-gather.11.cloned.1.call-done = bf16[1024,2048]{0,1:T(8,128)(2,1)} async-done(((bf16[1024,16]{0,1:T(8,128)(2,1)}), bf16[1024,2048]{0,1:T(8,128)(2,1)}) %all-gather.11.cloned.1.call-update) | async-done | bytes 4194320 | tf_op jit(solution)/shard_map/all_gather | solution.py:90
  376.8 130.7 %all-gather.9.cloned.1.call-done = bf16[2048,1024]{1,0:T(8,128)(2,1)} async-done(((bf16[16,1024]{1,0:T(8,128)(2,1)}), bf16[2048,1024]{1,0:T(8,128)(2,1)}) %all-gather.9.cloned.1.call-update) | async-done | bytes 4194320 | tf_op jit(solution)/shard_map/all_gather | solution.py:85
  507.5 0.0 copy-done.2
  507.5 7.1 %convolution_convert_fusion = bf16[256,2048]{0,1:T(8,128)(2,1)} fusion(bf16[1024,2048]{0,1:T(8,128)(2,1)} %all-gather.11.cloned.1.call-done, bf16[256,2048]{0,1:T(8,128)(2,1)S(1)} %copy-done.2, bf16[2048,1024]{1,0:T(8,128)(2,1)} %all-gather.9.cloned.1.call-done, f32[256,1024]{1,0:T(8,128)S(1)} %fusion.62), kind=kOutput, calls=%fused_computation | convolution fusion | flops 2149580800 | bytes 11534336 | tf_op jit(solution)/shard_map/dot_general | solution.py:91
  514.6 0.0 all-reduce.2.cloned.1.call-update
  514.7 0.8 copy.13
  515.5 50.4 %all-reduce.2.cloned.1.call-done = bf16[256,2048]{0,1:T(8,128)(2,1)} async-done(((bf16[256,2048]{0,1:T(8,128)(2,1)}), bf16[256,2048]{0,1:T(8,128)(2,1)}) %all-reduce.2.cloned.1.call-update) | async-done | bytes 1048592 | tf_op jit(solution)/shard_map/psum | solution.py:93
  565.9 1.0 convert_add_fusion
  566.9 1.0 copy.14
  (15 shorter events, 0.2 us)
Async XLA Ops:
  7.2 38.1 %copy-start.3 = (bf16[256,512]{1,0:T(8,128)(2,1)S(1)}, bf16[256,512]{1,0:T(8,128)(2,1)}, u32[]{:S(2)}) copy-start(bf16[256,512]{1,0:T(8,128)(2,1)} %param.12) | copy-start | bytes 786436
  7.2 106.5 %all-gather.5.cloned.1.call-start = ((), (), s32[]{:S(2)}) async-start(), calls=%async_computation | async-start | bytes 1310720 | tf_op jit(solution)/shard_map/all_gather | solution.py:82
  9.9 26.4 %collective-permute-start = (bf16[256]{0:T(256)(128)(2,1)S(1)}, bf16[256]{0:T(256)(128)(2,1)S(1)}, u32[]{:S(2)}, u32[]{:S(2)}) collective-permute-start(bf16[256]{0:T(256)(128)(2,1)S(1)} %get-tuple-element.21), channel_id=1, source_target_pairs={{0,8},{4,12},{8,16},{12,20},{16,24},{20,28},{24,32},{28,36},{32,40... | collective-permute-start | bytes 1544 | tf_op jit(solution)/shard_map/ppermute | solution.py:17
  18.2 22.3 %collective-permute-start.1 = (bf16[256]{0:T(256)(128)(2,1)S(1)}, bf16[256]{0:T(256)(128)(2,1)S(1)}, u32[]{:S(2)}, u32[]{:S(2)}) collective-permute-start(bf16[256]{0:T(256)(128)(2,1)S(1)} %get-tuple-element.21), channel_id=1, source_target_pairs={{0,4},{4,8},{8,12},{12,16},{16,20},{20,24},{24,28},{28,32},{32,36}... | collective-permute-start | bytes 1544 | tf_op jit(solution)/shard_map/ppermute | solution.py:17
  20.6 19.9 %collective-permute-start.2 = (bf16[256,512]{1,0:T(8,128)(2,1)}, bf16[256,512]{1,0:T(8,128)(2,1)S(1)}, u32[]{:S(2)}, u32[]{:S(2)}) collective-permute-start(bf16[256,512]{1,0:T(8,128)(2,1)} %param.13), channel_id=1, source_target_pairs={{0,8},{4,12},{8,16},{12,20},{16,24},{20,28},{24,32},{28,36},{32,40... | collective-permute-start | bytes 786440 | tf_op jit(solution)/shard_map/ppermute | solution.py:17
  26.0 17.0 %collective-permute-start.3 = (bf16[256,512]{1,0:T(8,128)(2,1)}, bf16[256,512]{1,0:T(8,128)(2,1)S(1)}, u32[]{:S(2)}, u32[]{:S(2)}) collective-permute-start(bf16[256,512]{1,0:T(8,128)(2,1)} %param.13), channel_id=1, source_target_pairs={{0,4},{4,8},{8,12},{12,16},{16,20},{20,24},{24,28},{28,32},{32,36}... | collective-permute-start | bytes 786440 | tf_op jit(solution)/shard_map/ppermute | solution.py:17
  31.4 17.8 %collective-permute-start.4 = (bf16[256,512]{1,0:T(8,128)(2,1)}, bf16[256,512]{1,0:T(8,128)(2,1)S(1)}, u32[]{:S(2)}, u32[]{:S(2)}) collective-permute-start(bf16[256,512]{1,0:T(8,128)(2,1)} %param.14), channel_id=1, source_target_pairs={{0,8},{4,12},{8,16},{12,20},{16,24},{20,28},{24,32},{28,36},{32,40... | collective-permute-start | bytes 786440 | tf_op jit(solution)/shard_map/ppermute | solution.py:17
  36.3 23.5 %collective-permute-start.5 = (bf16[256,512]{1,0:T(8,128)(2,1)}, bf16[256,512]{1,0:T(8,128)(2,1)S(1)}, u32[]{:S(2)}, u32[]{:S(2)}) collective-permute-start(bf16[256,512]{1,0:T(8,128)(2,1)} %param.14), channel_id=1, source_target_pairs={{0,4},{4,8},{8,12},{12,16},{16,20},{20,24},{24,28},{28,32},{32,36}... | collective-permute-start | bytes 786440 | tf_op jit(solution)/shard_map/ppermute | solution.py:17
  43.9 15.9 %copy-start = (bf16[256,512]{1,0:T(8,128)(2,1)S(1)}, bf16[256,512]{1,0:T(8,128)(2,1)}, u32[]{:S(2)}) copy-start(bf16[256,512]{1,0:T(8,128)(2,1)} %param.14) | copy-start | bytes 786436
  61.5 19.2 %copy-start.1 = (f32[512]{0:T(512)S(1)}, f32[512]{0:T(512)}, u32[]{:S(2)}) copy-start(f32[512]{0:T(512)} %param.16) | copy-start | bytes 6148
  81.6 164.3 %all-gather.7.cloned.1.call-start = ((), (), s32[]{:S(2)}) async-start(), calls=%async_computation.1 | async-start | bytes 4227072 | tf_op jit(solution)/shard_map/all_gather | solution.py:84
  82.4 294.4 %all-gather.11.cloned.1.call-start = ((), (), s32[]{:S(2)}) async-start(), calls=%async_computation.3 | async-start | bytes 4227072 | tf_op jit(solution)/shard_map/all_gather | solution.py:90
  83.1 424.4 %all-gather.9.cloned.1.call-start = ((), (), s32[]{:S(2)}) async-start(), calls=%async_computation.2 | async-start | bytes 4227072 | tf_op jit(solution)/shard_map/all_gather | solution.py:85
  83.7 482.2 %all-reduce.2.cloned.1.call-start = ((), (), s32[]{:S(2)}) async-start(), calls=%async_computation.4 | async-start | bytes 2097152 | tf_op jit(solution)/shard_map/psum | solution.py:93
  113.7 393.9 %copy-start.2 = (bf16[256,2048]{0,1:T(8,128)(2,1)S(1)}, bf16[256,2048]{0,1:T(8,128)(2,1)}, u32[]{:S(2)}) copy-start(bf16[256,2048]{0,1:T(8,128)(2,1)} %all-gather.5.cloned.1.call-done) | copy-start | bytes 3145732
Sparse Core Ops, SparseCore 0:
  81.7 31.8 all-gather.4
  118.2 127.7 all-gather.6
  250.5 126.2 all-gather.10
  381.2 126.2 all-gather.8
  514.7 51.0 all-reduce.1
where the time goes:
time: 575 us; the launch traced here: 574 us
  waiting for transfers between devices  488 us (85%)
  starting transfers between devices  29.5 us (5%)
  blocking collectives  17.3 us (3%)
  matrix products  15.9 us (3%)
  between operations  14.1 us (2%)
    all_gather x1, waiting for transfers between devices, on_device(): lax.all_gather(gate_weight, 'seq', axis=0, tiled=True)  132 us
    all_gather x1, waiting for transfers between devices, on_device(): lax.all_gather(up_weight, 'seq', axis=0, tiled=True)  131 us
    all_gather x1, waiting for transfers between devices, on_device(): down_full = lax.all_gather(down_weight, 'seq', axis=1, tiled=True)  127 us
    psum x1, waiting for transfers between devices, on_device(): lax.psum(partial_value.astype(jnp.bfloat16), 'tp').astype(jnp.float32)  50.4 us
    all_gather x1, waiting for transfers between devices, on_device(): normed_full = lax.all_gather(normed, 'tp', axis=1, tiled=True)  29.9 us
    ppermute x6, starting transfers between devices, from_behind(): return lax.ppermute(value, axis, pairs)  29.3 us
    psum x1, blocking collectives, on_device(): square_sum = lax.psum(jnp.sum(residual * residual, axis=1), 'tp')  17.3 us
    ppermute x6, waiting for transfers between devices, from_behind(): return lax.ppermute(value, axis, pairs)  15.6 us
  transfers between devices with their start and end apart: 11, of which 8 were waited for; matrix products, arithmetic and copies ran while one was open for 2% of the time, Pallas kernels for 0%

commit v1 on v0

--- a/solution.py
+++ b/solution.py
@@ -87,7 +87,9 @@
     gate_sum = jnp.dot(normed_full, gate_full, preferred_element_type=jnp.float32)
     up_sum = jnp.dot(normed_full, up_full, preferred_element_type=jnp.float32)
     hidden = (jax.nn.silu(gate_sum) * up_sum).astype(jnp.bfloat16)
-    down_full = lax.all_gather(down_weight, "seq", axis=1, tiled=True)
+    down_full = jnp.concatenate(
+        lax.all_to_all(jnp.stack([down_weight] * lax.axis_size("seq")), "seq", 0, 0), axis=1
+    )
     partial_value = jnp.dot(hidden, down_full, preferred_element_type=jnp.float32)
     tp_width = residual_in.shape[1]
     summed = lax.psum(partial_value.astype(jnp.bfloat16), "tp").astype(jnp.float32)

time: 575 us -> 507 us (0.88)
  waiting for transfers between devices: 488 us -> 397 us
  starting transfers between devices: 29.5 us -> 49.4 us
    all_gather x1 -> x0, waiting for transfers between devices: 127 us -> none  [on_device(): down_full = lax.all_gather(down_weight, 'seq', axis=1, tiled=True)]
    all_gather x1, waiting for transfers between devices: 132 us -> 162 us  [on_device(): lax.all_gather(gate_weight, 'seq', axis=0, tiled=True)]
    all_to_all x0 -> x1, starting transfers between devices: none -> 20 us  [on_device(): lax.all_to_all(jnp.stack([down_weight] * lax.axis_size('seq')), 'seq', 0, 0)]
    all_gather x1, waiting for transfers between devices: 29.9 us -> 40.4 us  [on_device(): normed_full = lax.all_gather(normed, 'tp', axis=1, tiled=True)]
  transfers between devices with their start and end apart: 11 -> 11, of which waited for: 8 -> 7; matrix products, arithmetic and copies ran while one was open for 2% -> 2% of each run, Pallas kernels for 0% -> 0%
where the time goes in v1:
time: 507 us; the launch traced here: 506 us
  waiting for transfers between devices  397 us (78%)
  starting transfers between devices  49.4 us (10%)
  blocking collectives  17.3 us (3%)
  matrix products  15.9 us (3%)
  between operations  14.1 us (3%)
  local copies, waits for them, and re-layouts  7.97 us (2%)
    all_gather x1, waiting for transfers between devices, on_device(): lax.all_gather(gate_weight, 'seq', axis=0, tiled=True)  162 us
    all_gather x1, waiting for transfers between devices, on_device(): lax.all_gather(up_weight, 'seq', axis=0, tiled=True)  127 us
    psum x1, waiting for transfers between devices, on_device(): lax.psum(partial_value.astype(jnp.bfloat16), 'tp').astype(jnp.float32)  50.4 us
    all_gather x1, waiting for transfers between devices, on_device(): normed_full = lax.all_gather(normed, 'tp', axis=1, tiled=True)  40.4 us
    ppermute x6, starting transfers between devices, from_behind(): return lax.ppermute(value, axis, pairs)  29.3 us
    all_to_all x1, starting transfers between devices, on_device(): lax.all_to_all(jnp.stack([down_weight] * lax.axis_size('seq')), 'seq', 0, 0)  20 us
    psum x1, blocking collectives, on_device(): square_sum = lax.psum(jnp.sum(residual * residual, axis=1), 'tp')  17.3 us
    ppermute x6, waiting for transfers between devices, from_behind(): return lax.ppermute(value, axis, pairs)  15.6 us
  transfers between devices with their start and end apart: 11, of which 7 were waited for; matrix products, arithmetic and copies ran while one was open for 2% of the time, Pallas kernels for 0%

profile of v1, /device:TPU:1, one launch (start us, length us, event | category | flops | bytes accessed | tf_op | source)
XLA Modules:
  0.0 506.1 jit_solution(1237730198919685634)
XLA Ops:
  7.2 0.0 copy-start.4
  7.2 0.0 all-gather.4.cloned.1.call-start
  7.2 1.3 fusion.57
  8.6 1.3 compare_select_fusion.1
  9.9 8.3 %collective-permute-start = (bf16[256]{0:T(256)(128)(2,1)S(1)}, bf16[256]{0:T(256)(128)(2,1)S(1)}, u32[]{:S(2)}, u32[]{:S(2)}) collective-permute-start(bf16[256]{0:T(256)(128)(2,1)S(1)} %get-tuple-element.23), channel_id=1, source_target_pairs={{0,8},{4,12},{8,16},{12,20},{16,24},{20,28},{24,32},{28,36},{32,40... | collective-permute-start | bytes 1544 | tf_op jit(solution)/shard_map/ppermute | solution.py:17
  18.2 2.4 collective-permute-start.1
  20.6 5.4 %collective-permute-start.2 = (bf16[256,512]{1,0:T(8,128)(2,1)}, bf16[256,512]{1,0:T(8,128)(2,1)S(1)}, u32[]{:S(2)}, u32[]{:S(2)}) collective-permute-start(bf16[256,512]{1,0:T(8,128)(2,1)} %param.13), channel_id=1, source_target_pairs={{0,8},{4,12},{8,16},{12,20},{16,24},{20,28},{24,32},{28,36},{32,40... | collective-permute-start | bytes 786440 | tf_op jit(solution)/shard_map/ppermute | solution.py:17
  26.0 5.4 %collective-permute-start.3 = (bf16[256,512]{1,0:T(8,128)(2,1)}, bf16[256,512]{1,0:T(8,128)(2,1)S(1)}, u32[]{:S(2)}, u32[]{:S(2)}) collective-permute-start(bf16[256,512]{1,0:T(8,128)(2,1)} %param.13), channel_id=1, source_target_pairs={{0,4},{4,8},{8,12},{12,16},{16,20},{20,24},{24,28},{28,32},{32,36}... | collective-permute-start | bytes 786440 | tf_op jit(solution)/shard_map/ppermute | solution.py:17
  31.4 3.5 collective-permute-start.4
  35.0 1.2 copy.16
  36.3 0.0 collective-permute-done
  36.3 4.2 collective-permute-start.5
  40.5 0.0 collective-permute-done.1
  40.5 0.0 collective-permute-done.2
  40.6 2.4 collective-permute-done.3
  43.0 1.0 constant_dynamic-update-slice_fusion
  43.9 0.0 copy-start
  43.9 1.3 fusion.59
  45.2 0.0 copy-done.4
  45.3 0.4 fusion.60
  45.7 0.4 fusion.61
  46.1 3.1 collective-permute-done.4
  49.2 0.4 fusion.58
  49.6 10.2 %collective-permute-done.5 = bf16[256,512]{1,0:T(8,128)(2,1)S(1)} collective-permute-done((bf16[256,512]{1,0:T(8,128)(2,1)}, bf16[256,512]{1,0:T(8,128)(2,1)S(1)}, u32[]{:S(2)}, u32[]{:S(2)}) %collective-permute-start.5) | collective-permute-done | bytes 262176 | tf_op jit(solution)/shard_map/ppermute | solution.py:17
  59.8 0.0 copy-done
  59.8 1.0 fusion.17
  60.9 0.6 fusion.13
  61.5 0.0 copy-start.2
  61.5 0.6 fusion.14
  62.1 0.0 copy-start.1
  62.1 0.6 fusion.15
  62.8 0.6 fusion.16
  63.4 0.1 multiply_reduce_fusion
  63.5 17.3 %psum.14 = f32[256]{0:T(256)S(1)} all-reduce(f32[256]{0:T(256)S(1)} %multiply_reduce_fusion), channel_id=1, replica_groups=mesh['seq'=128,'tp'=4] {'tp'}, use_global_device_ids=true, to_apply=%region_9.10 | all-reduce | flops 256 | bytes 2048 | tf_op jit(solution)/shard_map/psum | solution.py:79
  80.8 0.0 copy-done.2
  80.8 0.8 multiply_convert_fusion
  81.6 0.0 all-gather.4.cloned.1.call-update
  81.6 0.0 all-gather.6.cloned.1.call-start
  81.7 0.7 all-gather.6.cloned.1.call-update
  82.4 0.0 all-gather.8.cloned.1.call-start
  82.4 0.7 all-gather.8.cloned.1.call-update
  83.1 0.0 copy-done.1
  83.1 2.5 stack.2
  85.6 20.0 %all-to-all-start = ((bf16[128,1024,16]{1,2,0:T(8,128)(2,1)}), bf16[128,1024,16]{1,2,0:T(8,128)(2,1)}, u32[]{:S(2)}, u32[]{:S(2)}) async-start(bf16[128,1024,16]{1,2,0:T(8,128)(2,1)} %stack.2), calls=%async_computation | async-start | bytes 8388608 | tf_op jit(solution)/shard_map/all_to_all | solution.py:91
  105.6 0.0 all-reduce.2.cloned.1.call-start
  105.6 40.4 %all-gather.4.cloned.1.call-done = bf16[256,2048]{0,1:T(8,128)(2,1)} async-done(((bf16[256,512]{0,1:T(8,128)(2,1)}), bf16[256,2048]{0,1:T(8,128)(2,1)}) %all-gather.4.cloned.1.call-update) | async-done | bytes 1048592 | tf_op jit(solution)/shard_map/all_gather | solution.py:82
  146.0 0.0 copy-start.3
  146.0 162.2 %all-gather.6.cloned.1.call-done = bf16[2048,1024]{1,0:T(8,128)(2,1)} async-done(((bf16[16,1024]{1,0:T(8,128)(2,1)}), bf16[2048,1024]{1,0:T(8,128)(2,1)}) %all-gather.6.cloned.1.call-update) | async-done | bytes 4194320 | tf_op jit(solution)/shard_map/all_gather | solution.py:84
  308.3 3.8 fusion.62
  312.1 127.1 %all-gather.8.cloned.1.call-done = bf16[2048,1024]{1,0:T(8,128)(2,1)} async-done(((bf16[16,1024]{1,0:T(8,128)(2,1)}), bf16[2048,1024]{1,0:T(8,128)(2,1)}) %all-gather.8.cloned.1.call-update) | async-done | bytes 4194320 | tf_op jit(solution)/shard_map/all_gather | solution.py:85
  439.1 0.0 all-to-all-done
  439.1 0.0 copy-done.3
  439.1 7.1 %convolution_convert_fusion = bf16[256,2048]{0,1:T(8,128)(2,1)} fusion(bf16[1024,2048]{0,1:T(8,128)(2,1)} %bitcast.12, bf16[256,2048]{0,1:T(8,128)(2,1)S(1)} %copy-done.3, bf16[2048,1024]{1,0:T(8,128)(2,1)} %all-gather.8.cloned.1.call-done, f32[256,1024]{1,0:T(8,128)S(1)} %fusion.62), kind=kOutput, calls=%fused_computation | convolution fusion | flops 2149580800 | bytes 11534336 | tf_op jit(solution)/shard_map/dot_general | solution.py:93
  446.2 0.0 all-reduce.2.cloned.1.call-update
  446.3 0.8 copy.18
  447.1 50.4 %all-reduce.2.cloned.1.call-done = bf16[256,2048]{0,1:T(8,128)(2,1)} async-done(((bf16[256,2048]{0,1:T(8,128)(2,1)}), bf16[256,2048]{0,1:T(8,128)(2,1)}) %all-reduce.2.cloned.1.call-update) | async-done | bytes 1048592 | tf_op jit(solution)/shard_map/psum | solution.py:95
  497.5 1.0 convert_add_fusion
  498.5 1.0 copy.19
  (15 shorter events, 0.2 us)
Async XLA Ops:
  7.2 38.1 %copy-start.4 = (bf16[256,512]{1,0:T(8,128)(2,1)S(1)}, bf16[256,512]{1,0:T(8,128)(2,1)}, u32[]{:S(2)}) copy-start(bf16[256,512]{1,0:T(8,128)(2,1)} %param.12) | copy-start | bytes 786436
  7.2 138.8 %all-gather.4.cloned.1.call-start = ((), (), s32[]{:S(2)}) async-start(), calls=%async_computation.1 | async-start | bytes 1310720 | tf_op jit(solution)/shard_map/all_gather | solution.py:82
  9.9 26.4 %collective-permute-start = (bf16[256]{0:T(256)(128)(2,1)S(1)}, bf16[256]{0:T(256)(128)(2,1)S(1)}, u32[]{:S(2)}, u32[]{:S(2)}) collective-permute-start(bf16[256]{0:T(256)(128)(2,1)S(1)} %get-tuple-element.23), channel_id=1, source_target_pairs={{0,8},{4,12},{8,16},{12,20},{16,24},{20,28},{24,32},{28,36},{32,40... | collective-permute-start | bytes 1544 | tf_op jit(solution)/shard_map/ppermute | solution.py:17
  18.2 22.3 %collective-permute-start.1 = (bf16[256]{0:T(256)(128)(2,1)S(1)}, bf16[256]{0:T(256)(128)(2,1)S(1)}, u32[]{:S(2)}, u32[]{:S(2)}) collective-permute-start(bf16[256]{0:T(256)(128)(2,1)S(1)} %get-tuple-element.23), channel_id=1, source_target_pairs={{0,4},{4,8},{8,12},{12,16},{16,20},{20,24},{24,28},{28,32},{32,36}... | collective-permute-start | bytes 1544 | tf_op jit(solution)/shard_map/ppermute | solution.py:17
  20.6 19.9 %collective-permute-start.2 = (bf16[256,512]{1,0:T(8,128)(2,1)}, bf16[256,512]{1,0:T(8,128)(2,1)S(1)}, u32[]{:S(2)}, u32[]{:S(2)}) collective-permute-start(bf16[256,512]{1,0:T(8,128)(2,1)} %param.13), channel_id=1, source_target_pairs={{0,8},{4,12},{8,16},{12,20},{16,24},{20,28},{24,32},{28,36},{32,40... | collective-permute-start | bytes 786440 | tf_op jit(solution)/shard_map/ppermute | solution.py:17
  26.0 17.0 %collective-permute-start.3 = (bf16[256,512]{1,0:T(8,128)(2,1)}, bf16[256,512]{1,0:T(8,128)(2,1)S(1)}, u32[]{:S(2)}, u32[]{:S(2)}) collective-permute-start(bf16[256,512]{1,0:T(8,128)(2,1)} %param.13), channel_id=1, source_target_pairs={{0,4},{4,8},{8,12},{12,16},{16,20},{20,24},{24,28},{28,32},{32,36}... | collective-permute-start | bytes 786440 | tf_op jit(solution)/shard_map/ppermute | solution.py:17
  31.4 17.8 %collective-permute-start.4 = (bf16[256,512]{1,0:T(8,128)(2,1)}, bf16[256,512]{1,0:T(8,128)(2,1)S(1)}, u32[]{:S(2)}, u32[]{:S(2)}) collective-permute-start(bf16[256,512]{1,0:T(8,128)(2,1)} %param.14), channel_id=1, source_target_pairs={{0,8},{4,12},{8,16},{12,20},{16,24},{20,28},{24,32},{28,36},{32,40... | collective-permute-start | bytes 786440 | tf_op jit(solution)/shard_map/ppermute | solution.py:17
  36.3 23.5 %collective-permute-start.5 = (bf16[256,512]{1,0:T(8,128)(2,1)}, bf16[256,512]{1,0:T(8,128)(2,1)S(1)}, u32[]{:S(2)}, u32[]{:S(2)}) collective-permute-start(bf16[256,512]{1,0:T(8,128)(2,1)} %param.14), channel_id=1, source_target_pairs={{0,4},{4,8},{8,12},{12,16},{16,20},{20,24},{24,28},{28,32},{32,36}... | collective-permute-start | bytes 786440 | tf_op jit(solution)/shard_map/ppermute | solution.py:17
  43.9 15.9 %copy-start = (bf16[256,512]{1,0:T(8,128)(2,1)S(1)}, bf16[256,512]{1,0:T(8,128)(2,1)}, u32[]{:S(2)}) copy-start(bf16[256,512]{1,0:T(8,128)(2,1)} %param.14) | copy-start | bytes 786436
  61.5 19.3 %copy-start.2 = (f32[512]{0:T(512)S(1)}, f32[512]{0:T(512)}, u32[]{:S(2)}) copy-start(f32[512]{0:T(512)} %param.16) | copy-start | bytes 6148
  62.1 21.0 %copy-start.1 = (bf16[1024,16]{0,1:T(8,128)(2,1)S(1)}, bf16[1024,16]{0,1:T(8,128)(2,1)}, u32[]{:S(2)}) copy-start(bf16[1024,16]{0,1:T(8,128)(2,1)} %param.19) | copy-start | bytes 98308
  81.6 226.6 %all-gather.6.cloned.1.call-start = ((), (), s32[]{:S(2)}) async-start(), calls=%async_computation.2 | async-start | bytes 4227072 | tf_op jit(solution)/shard_map/all_gather | solution.py:84
  82.4 356.7 %all-gather.8.cloned.1.call-start = ((), (), s32[]{:S(2)}) async-start(), calls=%async_computation.3 | async-start | bytes 4227072 | tf_op jit(solution)/shard_map/all_gather | solution.py:85
  85.6 353.5 %all-to-all-start = ((bf16[128,1024,16]{1,2,0:T(8,128)(2,1)}), bf16[128,1024,16]{1,2,0:T(8,128)(2,1)}, u32[]{:S(2)}, u32[]{:S(2)}) async-start(bf16[128,1024,16]{1,2,0:T(8,128)(2,1)} %stack.2), calls=%async_computation | async-start | bytes 8388608 | tf_op jit(solution)/shard_map/all_to_all | solution.py:91
  105.6 391.9 %all-reduce.2.cloned.1.call-start = ((), (), s32[]{:S(2)}) async-start(), calls=%async_computation.4 | async-start | bytes 2097152 | tf_op jit(solution)/shard_map/psum | solution.py:95
  146.0 293.1 %copy-start.3 = (bf16[256,2048]{0,1:T(8,128)(2,1)S(1)}, bf16[256,2048]{0,1:T(8,128)(2,1)}, u32[]{:S(2)}) copy-start(bf16[256,2048]{0,1:T(8,128)(2,1)} %all-gather.4.cloned.1.call-done) | copy-start | bytes 3145732
Sparse Core Ops, SparseCore 0:
  81.8 64.2 all-gather.3
  150.5 157.6 all-gather.5
  312.8 126.2 all-gather.7
  446.4 51.0 all-reduce.1
